TPU v7x, 32 devices: a whole 2x2x4 slice. The times are simulated.
32 devices in a mesh: groups: 1, ctx: 16 (over z, y, x), exp: 2 (over core).
Axes of the slice: x: 2, y: 2, z: 4, core: 2. Of those that a mesh axis runs over, the one named last changes fastest.
Arguments:
- queries: bfloat16 [2048, 2048], P(('groups', 'ctx'), 'exp'), may hold values from -40 to 40
- key_rows: bfloat16 [2048, 256], P(('groups', 'ctx'), 'exp'), may hold values from -15 to 15
- value_rows: bfloat16 [2048, 256], P(('groups', 'ctx'), 'exp'), may hold values from -6 to 6
- hidden_in: bfloat16 [2048, 1024], P(('groups', 'ctx')), may hold values from -40 to 40
- out_proj: bfloat16 [2048, 1024], P('exp'), may hold values from -0.125 to 0.125
- norm_gain: float32 [1024], replicated, may hold values from 0.1 to 1.9
- expert_ids: int32 [2048, 8], P(('groups', 'ctx')), may hold values from 0 to 15, all different within a row; in each aligned block of 128 rows (0 to 127, 128 to 255, ...) at most 96 rows name the same one
- gate_scores: float32 [2048, 8], P(('groups', 'ctx')), may hold values from 0.05 to 1
- w_gate: bfloat16 [16, 1024, 384], P('ctx'), may hold values from -0.1875 to 0.1875
- w_up: bfloat16 [16, 1024, 384], P('ctx'), may hold values from -0.1875 to 0.1875
- w_down: bfloat16 [16, 384, 1024], P('ctx'), may hold values from -0.3125 to 0.3125
Outputs:
- layer_out: bfloat16 [2048, 1024], P(('groups', 'ctx'), 'exp')
Inputs may be any that keep to these rules, and one draw needn't show every extreme that they name: `expert_ids`: each row names 8 different experts. No expert is named by more than 96 rows of one aligned block of 128 rows, a bound that some block reaches.
All inputs are finite; a program needn't handle non-finite values.
Results may differ from a plain program's by a relative error of at most 0.0035.
Values may be sent and summed in bfloat16 or wider, within the bound.
No kernel may reach another device: no remote copies, remote signals or barrier semaphores. Data moves between devices by JAX's collectives and lax.ppermute only.
A program may use at most 64 MiB of HBM per device.

v0:
```python
import math
import jax
import jax.numpy as jnp
from jax import lax
from jax.sharding import PartitionSpec as P


def attend(queries, key_rows, value_rows, first):
    token_count = queries.shape[0]
    kv_heads = key_rows.shape[1] // 128
    q_heads = queries.shape[1] // 128
    group = q_heads // kv_heads
    grouped = queries.reshape(token_count, kv_heads, group, 128)
    query_pos = first + jnp.arange(token_count, dtype=jnp.int32)
    last_pos = first + token_count - 1
    scale = 128 ** (-0.5)
    shape_rows = (kv_heads, group, token_count)
    start_state = (
        jnp.full(shape_rows, -1e30, jnp.float32),
        jnp.zeros(shape_rows, jnp.float32),
        jnp.zeros(shape_rows + (128,), jnp.float32),
    )
    key_piece = lax.all_gather(key_rows, "ctx", axis=0, tiled=True)
    value_piece = lax.all_gather(value_rows, "ctx", axis=0, tiled=True)
    count = key_piece.shape[0]
    width = math.gcd(count, 512)

    def step(block_index, state):
        offset = block_index * width

        def compute(inner):
            running_max, running_sum, accum = inner
            key_block = lax.dynamic_slice_in_dim(key_piece, block_index * width, width, 0).reshape(
                width, kv_heads, 128
            )
            value_block = lax.dynamic_slice_in_dim(
                value_piece, block_index * width, width, 0
            ).reshape(width, kv_heads, 128)
            scores = (
                jnp.einsum("tkgd,skd->kgts", grouped, key_block, preferred_element_type=jnp.float32)
                * scale
            )
            key_pos = offset + jnp.arange(width, dtype=jnp.int32)
            allowed = key_pos[None, :] <= query_pos[:, None]
            scores = jnp.where(allowed, scores, -jnp.inf)
            new_max = jnp.maximum(running_max, jnp.max(scores, axis=-1))
            factor = jnp.exp(running_max - new_max)
            weights = jnp.exp(scores - new_max[..., None])
            new_sum = running_sum * factor + jnp.sum(weights, axis=-1)
            product = jnp.einsum(
                "kgts,skd->kgtd",
                weights.astype(jnp.bfloat16),
                value_block,
                preferred_element_type=jnp.float32,
            )
            return (new_max, new_sum, accum * factor[..., None] + product)

        return lax.cond(offset <= last_pos, compute, lambda inner: inner, state)

    _, total, accum = lax.fori_loop(0, count // width, step, start_state)
    output = accum / total[..., None]
    return (
        jnp.transpose(output, (2, 0, 1, 3)).reshape(token_count, q_heads * 128).astype(jnp.bfloat16)
    )


def place_rows(expert_ids, sent_rows, capacity, expert_count):
    top_count = expert_ids.shape[1]
    flat_ids = expert_ids.reshape(-1)
    onehot = (flat_ids[:, None] == jnp.arange(expert_count, dtype=jnp.int32)[None, :]).astype(
        jnp.int32
    )
    earlier = jnp.cumsum(onehot, axis=0) - onehot
    slot_index = jnp.sum(earlier * onehot, axis=1)
    destination = flat_ids * capacity + slot_index
    copies = jnp.repeat(sent_rows, top_count, axis=0)
    buffer = (
        jnp.zeros((expert_count * capacity, sent_rows.shape[1]), sent_rows.dtype)
        .at[destination]
        .set(copies)
    )
    return (buffer.reshape(expert_count, 2, capacity // 2, sent_rows.shape[1]), destination)


def per_device(
    queries,
    key_rows,
    value_rows,
    hidden_in,
    out_proj,
    norm_gain,
    expert_ids,
    gate_scores,
    w_gate,
    w_up,
    w_down,
):
    token_count = queries.shape[0]
    model_width = hidden_in.shape[1]
    half_width = model_width // 2
    ctx_size = lax.axis_size("ctx")
    local_experts = w_gate.shape[0]
    expert_count = local_experts * ctx_size
    top_count = expert_ids.shape[1]
    capacity = 2 * (
        min(token_count, max(2, 3 * token_count * top_count // (2 * expert_count))) // 2
    )
    half_cap = capacity // 2
    first = lax.axis_index("ctx") * token_count
    core = lax.axis_index("exp")
    side_start = core * half_width
    attended = attend(queries, key_rows, value_rows, first)
    head_part = jnp.dot(attended, out_proj, preferred_element_type=jnp.float32)
    attn_full = lax.psum(head_part.astype(jnp.bfloat16), "exp").astype(jnp.float32)
    resid = hidden_in.astype(jnp.float32) + attn_full
    inverse = lax.rsqrt(jnp.mean(resid * resid, axis=1, keepdims=True) + 1e-06)
    sent_rows = (resid * inverse * norm_gain[None, :]).astype(jnp.bfloat16)
    resid_half = lax.dynamic_slice_in_dim(resid, side_start, half_width, 1)
    buffer, destination = place_rows(expert_ids, sent_rows, capacity, expert_count)
    own_slots = lax.dynamic_slice_in_dim(buffer, core, 1, 1)
    grouped = lax.all_to_all(own_slots, "ctx", split_axis=0, concat_axis=0, tiled=True)
    gate = jnp.einsum("sxmd,xdf->sxmf", grouped, w_gate, preferred_element_type=jnp.float32)
    upper = jnp.einsum("sxmd,xdf->sxmf", grouped, w_up, preferred_element_type=jnp.float32)
    hidden = (jax.nn.silu(gate) * upper).astype(jnp.bfloat16)
    partial_value = jnp.einsum(
        "sxmf,xfd->sxmd", hidden, w_down, preferred_element_type=jnp.float32
    ).astype(jnp.bfloat16)
    returned = lax.all_to_all(partial_value, "ctx", split_axis=0, concat_axis=0, tiled=True)
    flat_back = returned.reshape(expert_count * half_cap, model_width)
    slot_of = destination % capacity
    expert_of = destination // capacity
    owned = slot_of // half_cap == core
    local_index = jnp.where(owned, expert_of * half_cap + slot_of - core * half_cap, 0)
    picked = flat_back[local_index].astype(jnp.float32)
    mixing = (gate_scores / jnp.sum(gate_scores, axis=1, keepdims=True)).reshape(-1)
    mixing = jnp.where(owned, mixing, 0.0)
    weighted = (picked * mixing[:, None]).reshape(token_count, top_count, model_width)
    mixed_part = jnp.sum(weighted, axis=1)
    moe_half = lax.psum_scatter(
        mixed_part.astype(jnp.bfloat16), "exp", scatter_dimension=1, tiled=True
    ).astype(jnp.float32)
    return (resid_half + moe_half).astype(jnp.bfloat16)


def solution(mesh):
    placed = (
        P(("groups", "ctx"), "exp"),
        P(("groups", "ctx"), "exp"),
        P(("groups", "ctx"), "exp"),
        P(("groups", "ctx"), None),
        P("exp", None),
        P(),
        P(("groups", "ctx"), None),
        P(("groups", "ctx"), None),
        P("ctx", None, None),
        P("ctx", None, None),
        P("ctx", None, None),
    )
    return jax.shard_map(
        per_device,
        mesh=mesh,
        in_specs=placed,
        out_specs=P(("groups", "ctx"), "exp"),
        check_vma=False,
    )
```

profile of v0, /device:TPU:0, one launch (start us, length us, event | category | flops | bytes accessed | tf_op | source)
XLA Modules:
  0.0 254.2 jit_solution(11516045207703964452)
XLA Ops:
  6.5 0.0 copy-start
  6.5 0.0 all-reduce.2.cloned.1.call-start
  6.5 45.7 %all_gather.6 = bf16[2048,128]{1,0:T(8,128)(2,1)S(1)} all-gather(bf16[128,128]{1,0:T(8,128)(2,1)} %param.16), channel_id=1, replica_groups=mesh['groups'=1,'ctx'=16,'exp'=2] {'ctx'}, dimensions={0}, use_global_device_ids=true | all-gather | bytes 557056 | tf_op jit(solution)/shard_map/all_gather | solution.py:23
  52.2 40.9 %all_gather.7 = bf16[2048,128]{1,0:T(8,128)(2,1)} all-gather(bf16[128,128]{1,0:T(8,128)(2,1)} %param.17), channel_id=1, replica_groups=mesh['groups'=1,'ctx'=16,'exp'=2] {'ctx'}, dimensions={0}, use_global_device_ids=true | all-gather | bytes 557056 | tf_op jit(solution)/shard_map/all_gather | solution.py:24
  93.1 1.1 copy.47
  94.2 0.2 copy.48
  94.5 2.8 %while.18 = (s32[]{:T(128)}, f32[1,8,128]{2,1,0:T(8,128)S(1)}, f32[1,8,128]{2,1,0:T(8,128)S(1)}, f32[1,8,128,128]{3,2,1,0:T(8,128)S(1)}, s32[]{:T(128)}, /*index...) while((s32[]{:T(128)}, f32[1,8,128]{2,1,0:T(8,128)S(1)}, ...), condition=%wide.region_5.6_spmd.clone, body=%wide.region_0.5_spmd.clone.sunk | while | flops 272436864 | bytes 8067405 | solution.py:60
  94.5 2.6 %conditional.3 = ((f32[1,8,128]{2,1,0:T(8,128)S(1)}, f32[1,8,128]{2,1,0:T(8,128)S(1)}, f32[1,8,128,128]{3,2,1,0:T(8,128)S(1)})) conditional(s32[]{:T(128)} %convert_element_type.120, (f32[1,8,128]{2,1,0:T(8,128)S(1)}, f32[1,8,128]{2,1,0:T(8,128)S(1)}, f32[1,8,128,128]{3,2,1,0:T(8,128)S(1)}) %tuple.49, (s32[]{:T(128)}, s32[]{:T(128)}, s32[]{:T(128)}, ...), branch_computations={%region_1.0_spmd, %region_2.4_spmd} | conditional | flops 272436864 | bytes 8066654 | solution.py:58
  94.6 0.1 broadcast_compare_fusion
  94.7 0.4 fusion.55
  95.2 1.6 fusion.4
  96.8 0.3 fusion.3
  97.3 0.2 copy.49
  97.5 0.0 copy-start.3
  97.5 0.1 divide_convert_fusion
  97.6 0.0 copy-start.2
  97.6 0.0 copy-done
  97.6 0.0 copy-start.5
  97.6 1.2 convolution_convert_fusion.1
  98.8 0.0 all-reduce.2.cloned.1.call-update
  98.8 0.0 copy-done.3
  98.8 0.1 copy.51
  98.9 0.1 eq.51
  99.0 0.1 eq.47
  99.1 4.5 %reduce-window.6 = s32[16,8,128]{2,1,0:T(8,128)S(1)} reduce-window(s32[16,8,128]{2,1,0:T(8,128)S(1)} %fusion.51, s32[]{:T(128)} %constant.82.clone.1), window={size=1x1x128 pad=0_0x0_0x127_0}, to_apply=%region_7.8 | reduce-window | flops 2080768 | bytes 131076 | tf_op jit(solution)/shard_map/reduce-window
  103.7 0.1 slice.10
  103.7 0.1 copy.53
  103.9 0.1 copy.54
  104.0 0.1 broadcast_add_fusion.1
  104.1 0.1 copy.50
  104.2 0.1 mul.120
  104.3 0.1 compare_select_fusion
  104.4 18.4 %all-reduce.2.cloned.1.call-done = bf16[128,1024]{1,0:T(8,128)(2,1)} async-done(((bf16[128,1024]{1,0:T(8,128)(2,1)}), bf16[128,1024]{1,0:T(8,128)(2,1)}) %all-reduce.2.cloned.1.call-update) | async-done | bytes 262160 | tf_op jit(solution)/shard_map/psum | solution.py:114
  122.8 0.0 copy-done.2
  122.8 1.1 convert_add_fusion
  123.9 0.0 copy-done.5
  123.9 1.1 multiply_convert_fusion
  125.0 7.4 %scatter_custom_fusion = bf16[1536,1024]{1,0:T(8,128)(2,1)} fusion(s32[1024]{0:T(1024)S(1)} %bitcast.140, bf16[]{:T(256)} %constant.91.clone.1, bf16[128,1024]{1,0:T(8,128)(2,1)S(1)} %multiply_convert_fusion), kind=kCustom, calls=%fused_computation.27 | custom fusion | bytes 3407874 | tf_op jit(solution)/shard_map/scatter | solution.py:80
  132.4 1.6 constant_dynamic-slice_fusion
  133.9 0.0 copy-start.6
  133.9 44.7 %all_to_all.10 = bf16[16,1,48,1024]{3,2,1,0:T(8,128)(2,1)S(1)} all-to-all(bf16[16,1,48,1024]{3,2,1,0:T(8,128)(2,1)S(1)} %constant_dynamic-slice_fusion), channel_id=1, replica_groups=mesh['groups'=1,'ctx'=16,'exp'=2] {'ctx'}, dimensions={0} | all-to-all | bytes 3145728 | tf_op jit(solution)/shard_map/all_to_all | solution.py:121
  178.7 0.0 copy-start.1
  178.7 1.1 copy-done.1
  179.8 0.0 copy-done.6
  179.8 2.0 fusion.25
  181.8 5.2 %fusion.24 = bf16[16,1,48,1024]{3,2,1,0:T(8,128)(2,1)} fusion(bf16[16,1,48,1024]{3,2,1,0:T(8,128)(2,1)} %copy-done.1, f32[16,1,48,384]{3,2,0,1:T(8,128)} %fusion.25, bf16[1,384,1024]{2,1,0:T(8,128)(2,1)} %param.25, bf16[1,1024,384]{2,1,0:T(8,128)(2,1)} %param.24), kind=kOutput, calls=%fused_computation.35 | convolution fusion | flops 1210515456 | bytes 5898240 | tf_op jit(solution)/shard_map/sxmf,xfd->sxmd/dot_general | solution.py:125
  187.0 0.0 copy-start.4
  187.0 4.5 %all-to-all-start.1 = ((bf16[16,1,48,1024]{3,2,1,0:T(8,128)(2,1)}), bf16[16,1,48,1024]{3,2,1,0:T(8,128)(2,1)}, u32[]{:S(2)}, u32[]{:S(2)}) async-start(bf16[16,1,48,1024]{3,2,1,0:T(8,128)(2,1)} %fusion.24), calls=%async_computation.1 | async-start | bytes 3145728 | tf_op jit(solution)/shard_map/all_to_all | solution.py:128
  191.5 0.2 reduce-scatter.2.cloned.1.call-start
  191.8 0.1 reduce_sum.54
  191.9 0.0 copy-done.4
  192.0 0.1 copy.57
  192.1 32.7 %all-to-all-done.1 = bf16[16,1,48,1024]{3,2,1,0:T(8,128)(2,1)} async-done(((bf16[16,1,48,1024]{3,2,1,0:T(8,128)(2,1)}), bf16[16,1,48,1024]{3,2,1,0:T(8,128)(2,1)}, u32[]{:S(2)}, u32[]{:S(2)}) %all-to-all-start.1) | async-done | bytes 1572896 | tf_op jit(solution)/shard_map/all_to_all | solution.py:128
  224.8 7.6 %gather_fusion = bf16[1024,1024]{1,0:T(8,128)(2,1)} fusion(bf16[768,1024]{1,0:T(8,128)(2,1)} %bitcast.41, s32[1024]{0:T(1024)S(1)} %broadcast_clamp_fusion), kind=kCustom, calls=%fused_computation | custom fusion | bytes 4198400 | tf_op jit(solution)/shard_map/gather | solution.py:134
  232.4 3.7 %fusion.16 = bf16[128,1024]{1,0:T(8,128)(2,1)} fusion(bf16[1024,1024]{1,0:T(8,128)(2,1)} %gather_fusion, f32[128,8]{1,0:T(8,128)S(1)} %copy.57), kind=kLoop, calls=%fused_computation.26 | loop fusion | flops 3014656 | bytes 2363392 | tf_op jit(solution)/shard_map/reduce_sum | solution.py:138
  236.1 0.0 reduce-scatter.2.cloned.1.call-update
  236.1 9.7 %reduce-scatter.2.cloned.1.call-done = bf16[128,512]{1,0:T(8,128)(2,1)} async-done(((bf16[128,1024]{1,0:T(8,128)(2,1)}), bf16[128,512]{1,0:T(8,128)(2,1)}) %reduce-scatter.2.cloned.1.call-update) | async-done | bytes 131088 | tf_op jit(solution)/shard_map/reduce_scatter | solution.py:139
  245.8 1.6 add_convert_fusion
  (25 shorter events, 0.3 us)
Async XLA Ops:
  6.5 91.1 %copy-start = (bf16[1024,1024]{1,0:T(8,128)(2,1)S(1)}, bf16[1024,1024]{1,0:T(8,128)(2,1)}, u32[]{:S(2)}) copy-start(bf16[1024,1024]{1,0:T(8,128)(2,1)} %param.19) | copy-start | bytes 6291460
  6.5 116.2 %all-reduce.2.cloned.1.call-start = ((), (), s32[]{:S(2)}) async-start(), calls=%async_computation.3 | async-start | bytes 524288 | tf_op jit(solution)/shard_map/psum | solution.py:114
  97.5 1.3 copy-start.3
  97.6 25.2 %copy-start.2 = (bf16[128,1024]{1,0:T(8,128)(2,1)S(1)}, bf16[128,1024]{1,0:T(8,128)(2,1)}, u32[]{:S(2)}) copy-start(bf16[128,1024]{1,0:T(8,128)(2,1)} %param.18) | copy-start | bytes 786436
  97.6 26.3 %copy-start.5 = (f32[1024]{0:T(1024)S(1)}, f32[1024]{0:T(1024)}, u32[]{:S(2)}) copy-start(f32[1024]{0:T(1024)} %param.20) | copy-start | bytes 12292
  133.9 45.9 %copy-start.6 = (bf16[1,1024,384]{2,1,0:T(8,128)(2,1)S(1)}, bf16[1,1024,384]{2,1,0:T(8,128)(2,1)}, u32[]{:S(2)}) copy-start(bf16[1,1024,384]{2,1,0:T(8,128)(2,1)} %param.23) | copy-start | bytes 2359300
  178.7 1.1 copy-start.1
  187.0 4.9 %copy-start.4 = (f32[128,8]{0,1:T(8,128)S(1)}, f32[128,8]{0,1:T(8,128)}, u32[]{:S(2)}) copy-start(f32[128,8]{0,1:T(8,128)} %param.22) | copy-start | bytes 12292
  187.0 37.8 %all-to-all-start.1 = ((bf16[16,1,48,1024]{3,2,1,0:T(8,128)(2,1)}), bf16[16,1,48,1024]{3,2,1,0:T(8,128)(2,1)}, u32[]{:S(2)}, u32[]{:S(2)}) async-start(bf16[16,1,48,1024]{3,2,1,0:T(8,128)(2,1)} %fusion.24), calls=%async_computation.1 | async-start | bytes 3145728 | tf_op jit(solution)/shard_map/all_to_all | solution.py:128
  191.5 54.3 %reduce-scatter.2.cloned.1.call-start = ((), (), s32[]{:S(2)}) async-start(), calls=%async_computation.4 | async-start | bytes 393216 | tf_op jit(solution)/shard_map/reduce_scatter | solution.py:139
Sparse Core Ops, SparseCore 0:
  98.9 23.7 all-reduce.1
  236.3 9.4 reduce-scatter.1
where the time goes:
time: 255 us; the launch traced here: 254 us
  blocking collectives  131 us (51%)
  waiting for transfers between devices  60.8 us (24%)
  local copies, waits for them, and re-layouts  20.3 us (8%)
  between operations  13.6 us (5%)
  other arithmetic  12.8 us (5%)
  matrix products  10.4 us (4%)
  starting transfers between devices  4.76 us (2%)
    all_gather x1, blocking collectives, attend(): key_piece = lax.all_gather(key_rows, 'ctx', axis=0, tiled=True)  45.7 us
    all_to_all x1, blocking collectives, per_device(): lax.all_to_all(own_slots, 'ctx', split_axis=0, concat_axis=0, tiled=True)  44.7 us
    all_gather x1, blocking collectives, attend(): value_piece = lax.all_gather(value_rows, 'ctx', axis=0, tiled=True)  40.9 us
    all_to_all x1, waiting for transfers between devices, per_device(): lax.all_to_all(partial_value, 'ctx', split_axis=0, concat_axis=0, tiled=T...  32.7 us
    psum x1, waiting for transfers between devices, per_device(): lax.psum(head_part.astype(jnp.bfloat16), 'exp').astype(jnp.float32)  18.4 us
    reduce_scatter x1, waiting for transfers between devices, per_device(): lax.psum_scatter(mixed_part.astype(jnp.bfloat16), 'exp', scatter_dimensio...  9.66 us
    gather x1, local copies, waits for them, and re-layouts, per_device(): picked = flat_back[local_index].astype(jnp.float32)  7.65 us
    scatter x1, local copies, waits for them, and re-layouts, place_rows(): buffer = jnp.zeros((expert_count * capacity, sent_rows.shape[1]), sent_ro...  7.39 us
  transfers between devices with their start and end apart: 3, of which 3 were waited for; matrix products, arithmetic and copies ran while one was open for 2% of the time, Pallas kernels for 0%

commit v1 on v0

--- a/solution.py
+++ b/solution.py
@@ -111,7 +111,9 @@
     side_start = core * half_width
     attended = attend(queries, key_rows, value_rows, first)
     head_part = jnp.dot(attended, out_proj, preferred_element_type=jnp.float32)
-    attn_full = lax.psum(head_part.astype(jnp.bfloat16), "exp").astype(jnp.float32)
+    attn_full = jnp.sum(lax.all_gather(head_part.astype(jnp.bfloat16), "exp"), axis=0).astype(
+        jnp.float32
+    )
     resid = hidden_in.astype(jnp.float32) + attn_full
     inverse = lax.rsqrt(jnp.mean(resid * resid, axis=1, keepdims=True) + 1e-06)
     sent_rows = (resid * inverse * norm_gain[None, :]).astype(jnp.bfloat16)

time: 255 us -> 242 us (0.949)
  waiting for transfers between devices: 60.8 us -> 42.4 us
  blocking collectives: 131 us -> 138 us
    psum x1 -> x0, waiting for transfers between devices: 18.4 us -> none  [per_device(): lax.psum(head_part.astype(jnp.bfloat16), 'exp').astype(jnp.float32)]
    all_to_all x1, blocking collectives: 44.7 us -> 49 us  [per_device(): lax.all_to_all(own_slots, 'ctx', split_axis=0, concat_axis=0, tiled=True)]
  transfers between devices with their start and end apart: 3 -> 2, of which waited for: 3 -> 2; matrix products, arithmetic and copies ran while one was open for 2% -> 0% of each run, Pallas kernels for 0% -> 0%
where the time goes in v1:
time: 242 us; the launch traced here: 241 us
  blocking collectives  138 us (57%)
  waiting for transfers between devices  42.4 us (18%)
  local copies, waits for them, and re-layouts  21.2 us (9%)
  between operations  13.6 us (6%)
  other arithmetic  11.7 us (5%)
  matrix products  9.73 us (4%)
  starting transfers between devices  4.76 us (2%)
    all_to_all x1, blocking collectives, per_device(): lax.all_to_all(own_slots, 'ctx', split_axis=0, concat_axis=0, tiled=True)  49 us
    all_gather x1, blocking collectives, attend(): key_piece = lax.all_gather(key_rows, 'ctx', axis=0, tiled=True)  45.6 us
    all_gather x1, blocking collectives, attend(): value_piece = lax.all_gather(value_rows, 'ctx', axis=0, tiled=True)  40.9 us
    all_to_all x1, waiting for transfers between devices, per_device(): lax.all_to_all(partial_value, 'ctx', split_axis=0, concat_axis=0, tiled=T...  32.7 us
    reduce_scatter x1, waiting for transfers between devices, per_device(): lax.psum_scatter(mixed_part.astype(jnp.bfloat16), 'exp', scatter_dimensio...  9.66 us
    gather x1, local copies, waits for them, and re-layouts, per_device(): picked = flat_back[local_index].astype(jnp.float32)  7.65 us
    scatter x1, local copies, waits for them, and re-layouts, place_rows(): buffer = jnp.zeros((expert_count * capacity, sent_rows.shape[1]), sent_ro...  7.39 us
    dot_general x1, matrix products, per_device(): jnp.einsum('sxmf,xfd->sxmd', hidden, w_down, preferred_element_type=jnp.f...  5.18 us
  transfers between devices with their start and end apart: 2, of which 2 were waited for; matrix products, arithmetic and copies ran while one was open for 0% of the time, Pallas kernels for 0%

profile of v1, /device:TPU:0, one launch (start us, length us, event | category | flops | bytes accessed | tf_op | source)
XLA Modules:
  0.0 241.1 jit_solution(6577635150976122261)
XLA Ops:
  6.5 0.0 copy-start
  6.5 0.9 copy.51
  7.5 0.1 eq.51
  7.6 0.1 eq.47
  7.7 0.7 broadcast_multiply_fusion
  8.3 45.6 %all_gather.12 = bf16[2048,128]{1,0:T(8,128)(2,1)S(1)} all-gather(bf16[128,128]{1,0:T(8,128)(2,1)} %param.16), channel_id=1, replica_groups=mesh['groups'=1,'ctx'=16,'exp'=2] {'ctx'}, dimensions={0}, use_global_device_ids=true | all-gather | bytes 557056 | tf_op jit(solution)/shard_map/all_gather | solution.py:23
  53.9 40.9 %all_gather.13 = bf16[2048,128]{1,0:T(8,128)(2,1)} all-gather(bf16[128,128]{1,0:T(8,128)(2,1)} %param.17), channel_id=1, replica_groups=mesh['groups'=1,'ctx'=16,'exp'=2] {'ctx'}, dimensions={0}, use_global_device_ids=true | all-gather | bytes 557056 | tf_op jit(solution)/shard_map/all_gather | solution.py:24
  94.8 1.1 copy.47
  95.9 0.2 copy.48
  96.2 2.8 %while.18 = (s32[]{:T(128)}, f32[1,8,128]{2,1,0:T(8,128)S(1)}, f32[1,8,128]{2,1,0:T(8,128)S(1)}, f32[1,8,128,128]{3,2,1,0:T(8,128)S(1)}, s32[]{:T(128)}, /*index...) while((s32[]{:T(128)}, f32[1,8,128]{2,1,0:T(8,128)S(1)}, ...), condition=%wide.region_5.6_spmd.clone, body=%wide.region_0.5_spmd.clone.sunk | while | flops 272436864 | bytes 8067405 | solution.py:60
  96.2 2.6 %conditional.3 = ((f32[1,8,128]{2,1,0:T(8,128)S(1)}, f32[1,8,128]{2,1,0:T(8,128)S(1)}, f32[1,8,128,128]{3,2,1,0:T(8,128)S(1)})) conditional(s32[]{:T(128)} %convert_element_type.122, (f32[1,8,128]{2,1,0:T(8,128)S(1)}, f32[1,8,128]{2,1,0:T(8,128)S(1)}, f32[1,8,128,128]{3,2,1,0:T(8,128)S(1)}) %tuple.49, (s32[]{:T(128)}, s32[]{:T(128)}, s32[]{:T(128)}, ...), branch_computations={%region_1.0_spmd, %region_2.4_spmd} | conditional | flops 272436864 | bytes 8066654 | solution.py:58
  96.2 0.1 broadcast_compare_fusion
  96.4 0.4 fusion.55
  96.8 1.6 fusion.4
  98.5 0.3 fusion.3
  99.0 0.2 copy.49
  99.2 0.1 divide_convert_fusion
  99.2 0.0 copy-done
  99.2 0.0 copy-start.2
  99.3 0.5 convolution_convert_fusion.1
  99.7 0.0 copy-start.5
  99.8 2.2 all-gather
  101.9 0.1 reduce_sum.63
  102.0 0.0 copy-done.2
  102.0 0.2 convert_add_fusion
  102.2 4.5 %reduce-window.6 = s32[16,8,128]{2,1,0:T(8,128)S(1)} reduce-window(s32[16,8,128]{2,1,0:T(8,128)S(1)} %fusion.51, s32[]{:T(128)} %constant.83.clone.1), window={size=1x1x128 pad=0_0x0_0x127_0}, to_apply=%region_7.8 | reduce-window | flops 2080768 | bytes 131076 | tf_op jit(solution)/shard_map/reduce-window
  106.8 0.1 slice.10
  106.8 0.1 copy.53
  107.0 0.1 copy.54
  107.1 0.1 broadcast_add_fusion.1
  107.2 0.1 copy.50
  107.3 0.1 mul.120
  107.4 0.0 copy-done.5
  107.4 0.1 multiply_convert_fusion
  107.5 0.1 compare_select_fusion
  107.6 7.4 %scatter_custom_fusion = bf16[1536,1024]{1,0:T(8,128)(2,1)} fusion(s32[1024]{0:T(1024)S(1)} %bitcast.142, bf16[]{:T(256)} %constant.90.clone.1, bf16[128,1024]{1,0:T(8,128)(2,1)S(1)} %multiply_convert_fusion), kind=kCustom, calls=%fused_computation.27 | custom fusion | bytes 3407874 | tf_op jit(solution)/shard_map/scatter | solution.py:80
  115.0 1.6 constant_dynamic-slice_fusion
  116.6 0.0 copy-start.6
  116.6 49.0 %all_to_all.10 = bf16[16,1,48,1024]{3,2,1,0:T(8,128)(2,1)S(1)} all-to-all(bf16[16,1,48,1024]{3,2,1,0:T(8,128)(2,1)S(1)} %constant_dynamic-slice_fusion), channel_id=1, replica_groups=mesh['groups'=1,'ctx'=16,'exp'=2] {'ctx'}, dimensions={0} | all-to-all | bytes 3145728 | tf_op jit(solution)/shard_map/all_to_all | solution.py:123
  165.6 0.0 copy-start.1
  165.6 1.1 copy-done.1
  166.7 0.0 copy-done.6
  166.7 2.0 fusion.25
  168.7 5.2 %fusion.24 = bf16[16,1,48,1024]{3,2,1,0:T(8,128)(2,1)} fusion(bf16[16,1,48,1024]{3,2,1,0:T(8,128)(2,1)} %copy-done.1, f32[16,1,48,384]{3,2,0,1:T(8,128)} %fusion.25, bf16[1,384,1024]{2,1,0:T(8,128)(2,1)} %param.25, bf16[1,1024,384]{2,1,0:T(8,128)(2,1)} %param.24), kind=kOutput, calls=%fused_computation.35 | convolution fusion | flops 1210515456 | bytes 5898240 | tf_op jit(solution)/shard_map/sxmf,xfd->sxmd/dot_general | solution.py:127
  173.9 0.0 copy-start.4
  173.9 0.0 copy-start.3
  173.9 4.5 %all-to-all-start.1 = ((bf16[16,1,48,1024]{3,2,1,0:T(8,128)(2,1)}), bf16[16,1,48,1024]{3,2,1,0:T(8,128)(2,1)}, u32[]{:S(2)}, u32[]{:S(2)}) async-start(bf16[16,1,48,1024]{3,2,1,0:T(8,128)(2,1)} %fusion.24), calls=%async_computation.1 | async-start | bytes 3145728 | tf_op jit(solution)/shard_map/all_to_all | solution.py:130
  178.4 0.2 reduce-scatter.2.cloned.1.call-start
  178.7 0.1 reduce_sum.67
  178.8 0.0 copy-done.4
  178.8 0.0 copy-done.3
  178.9 0.1 copy.57
  179.0 32.7 %all-to-all-done.1 = bf16[16,1,48,1024]{3,2,1,0:T(8,128)(2,1)} async-done(((bf16[16,1,48,1024]{3,2,1,0:T(8,128)(2,1)}), bf16[16,1,48,1024]{3,2,1,0:T(8,128)(2,1)}, u32[]{:S(2)}, u32[]{:S(2)}) %all-to-all-start.1) | async-done | bytes 1572896 | tf_op jit(solution)/shard_map/all_to_all | solution.py:130
  211.7 7.6 %gather_fusion = bf16[1024,1024]{1,0:T(8,128)(2,1)} fusion(bf16[768,1024]{1,0:T(8,128)(2,1)} %bitcast.42, s32[1024]{0:T(1024)S(1)} %broadcast_clamp_fusion), kind=kCustom, calls=%fused_computation | custom fusion | bytes 4198400 | tf_op jit(solution)/shard_map/gather | solution.py:136
  219.4 3.7 %fusion.16 = bf16[128,1024]{1,0:T(8,128)(2,1)} fusion(bf16[1024,1024]{1,0:T(8,128)(2,1)} %gather_fusion, f32[128,8]{1,0:T(8,128)S(1)} %copy.57), kind=kLoop, calls=%fused_computation.26 | loop fusion | flops 3014656 | bytes 2363392 | tf_op jit(solution)/shard_map/reduce_sum | solution.py:140
  223.0 0.0 reduce-scatter.2.cloned.1.call-update
  223.1 9.7 %reduce-scatter.2.cloned.1.call-done = bf16[128,512]{1,0:T(8,128)(2,1)} async-done(((bf16[128,1024]{1,0:T(8,128)(2,1)}), bf16[128,512]{1,0:T(8,128)(2,1)}) %reduce-scatter.2.cloned.1.call-update) | async-done | bytes 131088 | tf_op jit(solution)/shard_map/reduce_scatter | solution.py:141
  232.7 1.6 add_convert_fusion
  (24 shorter events, 0.3 us)
Async XLA Ops:
  6.5 92.7 %copy-start = (bf16[1024,1024]{1,0:T(8,128)(2,1)S(1)}, bf16[1024,1024]{1,0:T(8,128)(2,1)}, u32[]{:S(2)}) copy-start(bf16[1024,1024]{1,0:T(8,128)(2,1)} %param.19) | copy-start | bytes 6291460
  99.2 2.8 %copy-start.2 = (bf16[128,1024]{1,0:T(8,128)(2,1)S(1)}, bf16[128,1024]{1,0:T(8,128)(2,1)}, u32[]{:S(2)}) copy-start(bf16[128,1024]{1,0:T(8,128)(2,1)} %param.18) | copy-start | bytes 786436
  99.7 7.6 %copy-start.5 = (f32[1024]{0:T(1024)S(1)}, f32[1024]{0:T(1024)}, u32[]{:S(2)}) copy-start(f32[1024]{0:T(1024)} %param.20) | copy-start | bytes 12292
  116.6 50.1 %copy-start.6 = (bf16[1,1024,384]{2,1,0:T(8,128)(2,1)S(1)}, bf16[1,1024,384]{2,1,0:T(8,128)(2,1)}, u32[]{:S(2)}) copy-start(bf16[1,1024,384]{2,1,0:T(8,128)(2,1)} %param.23) | copy-start | bytes 2359300
  165.6 1.1 copy-start.1
  173.9 4.9 %copy-start.4 = (f32[128,8]{0,1:T(8,128)S(1)}, f32[128,8]{0,1:T(8,128)}, u32[]{:S(2)}) copy-start(f32[128,8]{0,1:T(8,128)} %param.22) | copy-start | bytes 12292
  173.9 4.9 %copy-start.3 = (s32[128,8]{0,1:T(8,128)S(1)}, s32[128,8]{0,1:T(8,128)}, u32[]{:S(2)}) copy-start(s32[128,8]{0,1:T(8,128)} %param.21) | copy-start | bytes 12292
  173.9 37.8 %all-to-all-start.1 = ((bf16[16,1,48,1024]{3,2,1,0:T(8,128)(2,1)}), bf16[16,1,48,1024]{3,2,1,0:T(8,128)(2,1)}, u32[]{:S(2)}, u32[]{:S(2)}) async-start(bf16[16,1,48,1024]{3,2,1,0:T(8,128)(2,1)} %fusion.24), calls=%async_computation.1 | async-start | bytes 3145728 | tf_op jit(solution)/shard_map/all_to_all | solution.py:130
  178.4 54.3 %reduce-scatter.2.cloned.1.call-start = ((), (), s32[]{:S(2)}) async-start(), calls=%async_computation.3 | async-start | bytes 393216 | tf_op jit(solution)/shard_map/reduce_scatter | solution.py:141
Sparse Core Ops, SparseCore 0:
  223.2 9.4 reduce-scatter.1
